TPU v7x, 512 devices: a whole 4x8x8 slice. The times are simulated.
512 devices in a mesh: row: 16 (over x_lo, z), vec: 32 (over y, x_hi, core).
Axes of the slice: x: 4 (x_hi: 2, x_lo: 2; x = x_hi * 2 + x_lo), y: 8, z: 8, core: 2. Of those that a mesh axis runs over, the one named last changes fastest.
Arguments:
- vectors: float32 [16384, 16384], P('row', 'vec'), may hold values from -6 to 6
- block_index: int32 [3, 16], replicated, may hold values from 0 to 31
- block_offset: int32 [3, 16], replicated, may hold values from 0 to 3, as said below
- reflector_vectors: float32 [16, 32, 512, 256], P('row', 'vec'), may hold values from -0.25 to 0.25
- reflector_factors: float32 [16, 32, 256, 256], P('row', 'vec'), may hold values from -0.1875 to 0.1875
Outputs:
- updated: float32 [16384, 16384], P('row', 'vec')
Inputs may be any that keep to these rules, and one draw needn't show every extreme that they name: `block_offset`: the last owner's offset is at most 2, so every block lies inside the slab.
All inputs are finite; a program needn't handle non-finite values.
Results may differ from a plain program's by a relative error of at most 0.0001.
Values sent between devices are 32-bit elements; how exact they have to be, the bound alone decides.
A program may use at most 64 MiB of HBM per device.

v0:
```python
import functools

import jax
import jax.numpy as jnp
from jax import lax
from jax.experimental import pallas as pl
from jax.experimental.pallas import tpu as pltpu
from jax.sharding import PartitionSpec as P

MESH = pl.DeviceIdType.MESH
F32, BF16 = jnp.float32, jnp.bfloat16
FRONTS = 3
R = 256
H = 128
PACK = 704
NC = 4


def split(x):
    high = x.astype(BF16)
    return high, (x - high.astype(F32)).astype(BF16)


def where(value, target, yes, no):
    return jnp.where(jnp.full(yes.shape, value, jnp.int32) == jnp.full(yes.shape, target, jnp.int32), yes, no)


def mm(a, b):
    dot = functools.partial(jnp.dot, preferred_element_type=F32)
    return dot(a[0], b[0]) + (dot(a[0], b[1]) + dot(a[1], b[0]))


def kernel(
    n_row,
    n_vec,
    slab,
    index,
    offset,
    v_hbm,
    s_hbm,
    out,
    w,
    first,
    din,
    uout,
    uin,
    dout,
    pad,
    blk,
    sib_blk,
    vb,
    ps,
    pr,
    ms,
    mr,
    xs,
    xr,
    vt_h,
    vt_l,
    v_h,
    v_l,
    sx_h,
    sx_l,
    so_h,
    so_l,
    in_sem,
    raw_sem,
    p_ssem,
    p_rsem,
    m_ssem,
    m_rsem,
    x_ssem,
    x_rsem,
    ap_ssem,
    ap_rsem,
    am_ssem,
    am_rsem,
    c_ssem,
    c_rsem,
    u_ssem,
    u_rsem,
    d_ssem,
    d_rsem,
    out_sem,
):
    ny = n_vec // 4
    plus, minus = ny // 2, ny // 2 - 1
    rows = PACK // ny
    wide = w.shape[2]
    row, vec = lax.axis_index("row"), lax.axis_index("vec")
    y, half, core = vec // 4, (vec // 2) % 2, vec % 2
    up = (row, ((y + 1) % ny) * 4 + vec % 4)
    down = (row, ((y + ny - 1) % ny) * 4 + vec % 4)
    sib = (row, vec + 1 - 2 * core)
    across = (row, vec + 2 - 4 * half)
    below = ((row + 1) % n_row, vec)
    above = ((row + n_row - 1) % n_row, vec)
    other = 1 - core

    def remote(src, dst, ssem, rsem, to):
        return pltpu.make_async_remote_copy(
            src_ref=src, dst_ref=dst, send_sem=ssem, recv_sem=rsem, device_id=to, device_id_type=MESH
        )

    stage = [
        pltpu.make_async_copy(v_hbm.at[0, 0, :, pl.ds(0, H)], blk.at[0, pl.ds(0, 512)], in_sem.at[0]),
        pltpu.make_async_copy(v_hbm.at[0, 0, :, pl.ds(H, H)], blk.at[1, pl.ds(0, 512)], in_sem.at[1]),
        pltpu.make_async_copy(s_hbm.at[0, 0, pl.ds(0, 128), pl.ds(0, H)], blk.at[0, pl.ds(512, 128)], in_sem.at[2]),
        pltpu.make_async_copy(s_hbm.at[0, 0, pl.ds(192, 64), pl.ds(H, H)], blk.at[0, pl.ds(640, 64)], in_sem.at[3]),
        pltpu.make_async_copy(s_hbm.at[0, 0, pl.ds(0, 192), pl.ds(H, H)], blk.at[1, pl.ds(512, 192)], in_sem.at[4]),
    ]
    firsts = [
        pltpu.make_async_copy(slab.at[pl.ds(0, R), pl.ds(c * wide, wide)], first.at[c], in_sem.at[5 + c])
        for c in range(NC)
    ]
    loads = [
        pltpu.make_async_copy(slab.at[:, pl.ds(c * wide, wide)], w.at[c], in_sem.at[5 + NC + c]) for c in range(NC)
    ]
    for copy in stage + firsts + loads:
        copy.start()

    barrier = pltpu.get_barrier_semaphore()
    for to in (up, down, sib, across, below, above):
        pl.semaphore_signal(barrier, inc=1, device_id=to, device_id_type=MESH)
    pl.semaphore_wait(barrier, 6)

    for copy in stage:
        copy.wait()
    raw = remote(blk.at[other], sib_blk, raw_sem.at[0], raw_sem.at[1], sib)
    raw.start()

    def d_copy(k, src):
        return remote(src, din.at[k], d_ssem.at[k], d_rsem.at[k], above)

    for c in range(NC):
        firsts[c].wait()
        d_copy(c, first.at[c]).start()

    roots = [index[f, row] for f in range(FRONTS)]
    chip = [lax.shift_right_logical(root, 1) for root in roots]
    side = [lax.bitwise_and(part, 1) for part in chip]
    line = [lax.shift_right_logical(root, 2) for root in roots]

    def piece(o):
        return pl.ds(pl.multiple_of(o * rows, 8), rows)

    def candidate(f, o):
        return where(roots[f], sib[1], sib_blk[piece(o), :], blk[core, piece(o), :])

    def p_copy(f, s):
        i = f * plus + s
        return remote(ps.at[i], pr.at[i], p_ssem.at[i], p_rsem.at[i], up)

    def m_copy(f, s):
        i = f * minus + s
        return remote(ms.at[i], mr.at[i], m_ssem.at[i], m_rsem.at[i], down)

    def x_copy(f):
        return remote(xs.at[f], xr.at[f], x_ssem.at[f], x_rsem.at[f], across)

    def ap_copy(f, s):
        at = vb.at[f, core, piece((y + ny - s) % ny)]
        return remote(at, at, ap_ssem.at[f * plus + s], ap_rsem.at[f * plus + s], up)

    def ap_wait(f, s):
        at = vb.at[f, core, piece((y + ny - 1 - s) % ny)]
        remote(at, at, ap_ssem.at[f * plus + s], ap_rsem.at[f * plus + s], up).wait_recv()

    def am_copy(f, s):
        at = vb.at[f, core, piece((y + s) % ny)]
        return remote(at, at, am_ssem.at[f * minus + s], am_rsem.at[f * minus + s], down)

    def am_wait(f, s):
        at = vb.at[f, core, piece((y + 1 + s) % ny)]
        remote(at, at, am_ssem.at[f * minus + s], am_rsem.at[f * minus + s], down).wait_recv()

    def c_copy(f, t, o):
        at = vb.at[f, core, piece(o)]
        return remote(at, at, c_ssem.at[f * ny + t], c_rsem.at[f * ny + t], sib)

    def c_wait(f, t, o):
        at = vb.at[f, other, piece(o)]
        remote(at, at, c_ssem.at[f * ny + t], c_rsem.at[f * ny + t], sib).wait_recv()

    def slots():
        yield 0, y
        for s in range(plus):
            yield 1 + s, (y + ny - 1 - s) % ny
        for s in range(minus):
            yield 1 + plus + s, (y + 1 + s) % ny

    raw.wait_recv()
    for s in range(plus):
        for f in range(FRONTS):
            mine = candidate(f, (y + plus - s) % ny)
            if s > 0:
                p_copy(f, s - 1).wait_recv()
                mine = where(chip[f], vec // 2, mine, pr[f * plus + s - 1])
            ps[f * plus + s] = mine
            if s < minus:
                back = candidate(f, (y + ny - minus + s) % ny)
                if s > 0:
                    m_copy(f, s - 1).wait_recv()
                    back = where(chip[f], vec // 2, back, mr[f * minus + s - 1])
                ms[f * minus + s] = back
            p_copy(f, s).start()
            if s < minus:
                m_copy(f, s).start()
    for f in range(FRONTS):
        p_copy(f, plus - 1).wait_recv()
        m_copy(f, minus - 1).wait_recv()
        got = pr[f * plus + plus - 1]
        for s in range(minus):
            got = where(line[f], (y + 1 + s) % ny, mr[f * minus + minus - 1], got)
        xs[f] = where(chip[f], vec // 2, candidate(f, y), got)
        x_copy(f).start()
    for f in range(FRONTS):
        x_copy(f).wait_recv()
        vb[f, core, piece(y), :] = where(side[f], half, xs[f], xr[f])
        ap_copy(f, 0).start()
        am_copy(f, 0).start()
        c_copy(f, 0, y).start()
    for s in range(plus):
        for f in range(FRONTS):
            ap_wait(f, s)
            if s + 1 < plus:
                ap_copy(f, s + 1).start()
            c_copy(f, 1 + s, (y + ny - 1 - s) % ny).start()
            if s < minus:
                am_wait(f, s)
                if s + 1 < minus:
                    am_copy(f, s + 1).start()
                c_copy(f, 1 + plus + s, (y + 1 + s) % ny).start()
    for f in range(FRONTS):
        for t, o in slots():
            c_wait(f, t, o)

    def prepare(f):
        place = offset[f, row]
        for j in range(2):
            block = vb[f, j, 0:512, :]
            v_h[f, :, j * H : (j + 1) * H], v_l[f, :, j * H : (j + 1) * H] = split(block)
            vt_h[f, j * H : (j + 1) * H, :], vt_l[f, j * H : (j + 1) * H, :] = split(block.T)
        upper = lax.broadcasted_iota(jnp.int32, (H, H), 0) <= lax.broadcasted_iota(jnp.int32, (H, H), 1)
        a = jnp.where(upper, vb[f, 0, 512:640, :], 0.0)
        b = vb[f, 1, 512:640, :]
        c = jnp.where(upper, jnp.concatenate([vb[f, 1, 640:704, :], vb[f, 0, 640:704, :]], axis=0), 0.0)
        zero = jnp.zeros((H, H), F32)
        crossing = 3 + row // (n_row - 1)
        for i, j, part in ((0, 0, a), (0, 1, b), (1, 0, zero), (1, 1, c)):
            at = (f, slice(i * H, (i + 1) * H), slice(j * H, (j + 1) * H))
            high, low = split(where(place, crossing, part, zero))
            sx_h[at], sx_l[at] = high, low
            high, low = split(where(place, crossing, zero, part))
            so_h[at], so_l[at] = high, low

    for copy in loads:
        copy.wait()
    prepare(0)

    def u_copy(k):
        return remote(uout.at[k], uin.at[k], u_ssem.at[k], u_rsem.at[k], below)

    def cross(k):
        f, c = k // NC, k % NC
        d_copy(k, dout.at[0]).wait_recv()
        bottom, top = w[c, 3 * R : 4 * R, :], din[k]
        b, t = split(bottom), split(top)
        inner = mm((vt_h[f, :, 0:R], vt_l[f, :, 0:R]), b) + mm((vt_h[f, :, R : 2 * R], vt_l[f, :, R : 2 * R]), t)
        mixed = split(mm((sx_h[f], sx_l[f]), split(inner)))
        uout[k] = top - mm((v_h[f, R : 2 * R, :], v_l[f, R : 2 * R, :]), mixed)
        w[c, 3 * R : 4 * R, :] = bottom - mm((v_h[f, 0:R, :], v_l[f, 0:R, :]), mixed)
        u_copy(k).start()

    def out_copy(c):
        return pltpu.make_async_copy(w.at[c], out.at[:, pl.ds(c * wide, wide)], out_sem.at[c])

    def own(k):
        f, c = k // NC, k % NC
        place = offset[f, row]
        u_copy(k).wait_recv()
        parts = [uin[k]] + [w[c, b * R : (b + 1) * R, :] for b in range(1, 4)]
        window = [where(place, 0, parts[i], where(place, 1, parts[1 + i], parts[2 + i])) for i in range(2)]
        window = split(jnp.concatenate(window, axis=0))
        inner = mm((vt_h[f], vt_l[f]), window)
        mixed = split(mm((so_h[f], so_l[f]), split(inner)))
        pad[...] = mm((v_h[f], v_l[f]), mixed)
        none = jnp.zeros((R, wide), F32)

        def fresh(b):
            old = uin[k] if b == 0 else w[c, b * R : (b + 1) * R, :]
            lower = where(place, b - 1, pad[R : 2 * R, :], none) if b > 0 else none
            return old - where(place, b, pad[0:R, :], lower)

        top = fresh(0)
        w[c, 0:R, :] = top

        @pl.when(k < (FRONTS - 1) * NC)
        def _():
            dout[k] = top

        for b in range(1, 4):
            w[c, b * R : (b + 1) * R, :] = fresh(b)

        @pl.when(k < (FRONTS - 1) * NC)
        def _():
            d_copy(k + NC, dout.at[k]).start()

        @pl.when(k >= (FRONTS - 1) * NC)
        def _():
            pltpu.make_async_copy(
                w.at[c], out.at[:, pl.ds(pl.multiple_of(c * wide, wide), wide)], out_sem.at[c]
            ).start()

    def step(k, carry):
        @pl.when(k < FRONTS * NC)
        def _():
            cross(k)

        @pl.when(jnp.logical_or(k == 2, k == 3))
        def _():
            prepare(k - 1)

        @pl.when(k >= 2)
        def _():
            own(k - 2)

        return carry

    lax.fori_loop(0, FRONTS * NC + 2, step, 0)

    raw.wait_send()
    for f in range(FRONTS):
        x_copy(f).wait_send()
        for s in range(plus):
            p_copy(f, s).wait_send()
            ap_copy(f, s).wait_send()
        for s in range(minus):
            m_copy(f, s).wait_send()
            am_copy(f, s).wait_send()
        for t, o in slots():
            c_copy(f, t, o).wait_send()
    for k in range(FRONTS * NC):
        u_copy(k).wait_send()
        d_copy(k, dout.at[0]).wait_send()
    for c in range(NC):
        out_copy(c).wait()


def solution(mesh):
    n_row, n_vec = mesh.shape["row"], mesh.shape["vec"]
    ny = n_vec // 4
    plus, minus = ny // 2, ny // 2 - 1

    def body(vectors, block_index, block_offset, reflector_vectors, reflector_factors):
        wide = vectors.shape[1] // NC
        steps = FRONTS * NC
        dma = pltpu.SemaphoreType.DMA
        hbm, smem = pl.BlockSpec(memory_space=pl.ANY), pl.BlockSpec(memory_space=pltpu.SMEM)
        vmem = pltpu.VMEM
        rows = PACK // ny
        return pl.pallas_call(
            functools.partial(kernel, n_row, n_vec),
            out_shape=jax.ShapeDtypeStruct(vectors.shape, F32),
            in_specs=[hbm, smem, smem, hbm, hbm],
            out_specs=hbm,
            scratch_shapes=[
                vmem((NC, 4 * R, wide), F32),
                vmem((NC, R, wide), F32),
                vmem((steps, R, wide), F32),
                vmem((steps, R, wide), F32),
                vmem((steps, R, wide), F32),
                vmem((steps - NC, R, wide), F32),
                vmem((2 * R, wide), F32),
                vmem((2, PACK, H), F32),
                vmem((PACK, H), F32),
                vmem((FRONTS, 2, PACK, H), F32),
                vmem((FRONTS * plus, rows, H), F32),
                vmem((FRONTS * plus, rows, H), F32),
                vmem((FRONTS * minus, rows, H), F32),
                vmem((FRONTS * minus, rows, H), F32),
                vmem((FRONTS, rows, H), F32),
                vmem((FRONTS, rows, H), F32),
                vmem((FRONTS, R, 2 * R), BF16),
                vmem((FRONTS, R, 2 * R), BF16),
                vmem((FRONTS, 2 * R, R), BF16),
                vmem((FRONTS, 2 * R, R), BF16),
                vmem((FRONTS, R, R), BF16),
                vmem((FRONTS, R, R), BF16),
                vmem((FRONTS, R, R), BF16),
                vmem((FRONTS, R, R), BF16),
                dma((5 + 2 * NC,)),
                dma((2,)),
                dma((FRONTS * plus,)),
                dma((FRONTS * plus,)),
                dma((FRONTS * minus,)),
                dma((FRONTS * minus,)),
                dma((FRONTS,)),
                dma((FRONTS,)),
                dma((FRONTS * plus,)),
                dma((FRONTS * plus,)),
                dma((FRONTS * minus,)),
                dma((FRONTS * minus,)),
                dma((FRONTS * ny,)),
                dma((FRONTS * ny,)),
                dma((steps,)),
                dma((steps,)),
                dma((steps,)),
                dma((steps,)),
                dma((NC,)),
            ],
            compiler_params=pltpu.CompilerParams(
                collective_id=0, has_side_effects=True, vmem_limit_bytes=48 * 1024 * 1024
            ),
            name="fronts",
        )(vectors, block_index, block_offset, reflector_vectors, reflector_factors)

    return jax.shard_map(
        body,
        mesh=mesh,
        in_specs=(P("row", "vec"), P(), P(), P("row", "vec", None, None), P("row", "vec", None, None)),
        out_specs=P("row", "vec"),
        check_vma=False,
    )
```

profile of v0, /device:TPU:1, one launch (start us, length us, event | category | flops | bytes accessed | tf_op | source)
XLA Modules:
  0.0 102.0 jit_solution(17681298174045970807)
XLA Ops:
  0.0 0.0 copy-start
  0.0 1.6 %copy-done = f32[1024,512]{1,0:T(8,128)S(1)} copy-done((f32[1024,512]{1,0:T(8,128)S(1)}, f32[1024,512]{1,0:T(8,128)}, u32[]{:S(2)}) %copy-start) | copy-done | bytes 2097176
  1.6 0.0 copy-start.1
  1.6 1.0 %copy-done.1 = f32[1,1,512,256]{3,2,1,0:T(8,128)S(1)} copy-done((f32[1,1,512,256]{3,2,1,0:T(8,128)S(1)}, f32[1,1,512,256]{3,2,1,0:T(8,128)}, u32[]{:S(2)}) %copy-start.1) | copy-done | bytes 524312
  2.6 0.0 copy-start.2
  2.6 0.9 copy-done.2
  3.6 0.0 copy-start.3
  3.6 0.7 copy-done.3
  4.3 0.0 copy-start.4
  4.3 0.7 copy-done.4
  4.9 95.7 %fronts.1 = f32[1024,512]{1,0:T(8,128)S(1)} custom-call(f32[1024,512]{1,0:T(8,128)S(1)} %copy-done, s32[3,16]{1,0:T(4,128)S(1)} %copy-done.3, s32[3,16]{1,0:T(4,128)S(1)} %copy-done.4, f32[1,1,512,256]{3,2,1,0:T(8,128)S(1)} %copy-done.1, f32[1,1,256,256]{3,2,1,0:T(8,128)S(1)} %copy-done.2), custom_call_target="tpu_custom_call" | custom-call | tf_op jit(solution)/shard_map/fronts/pallas_call | solution.py:362
  100.6 1.3 %copy.7 = f32[1024,512]{1,0:T(8,128)} copy(f32[1024,512]{1,0:T(8,128)S(1)} %fronts.1) | data formatting | bytes 4194304
Async XLA Ops:
  0.0 1.6 %copy-start = (f32[1024,512]{1,0:T(8,128)S(1)}, f32[1024,512]{1,0:T(8,128)}, u32[]{:S(2)}) copy-start(f32[1024,512]{1,0:T(8,128)} %slab.1) | copy-start | bytes 6291460
  1.6 1.0 %copy-start.1 = (f32[1,1,512,256]{3,2,1,0:T(8,128)S(1)}, f32[1,1,512,256]{3,2,1,0:T(8,128)}, u32[]{:S(2)}) copy-start(f32[1,1,512,256]{3,2,1,0:T(8,128)} %v_hbm.1) | copy-start | bytes 1572868
  2.6 0.9 copy-start.2
  3.6 0.7 copy-start.3
  4.3 0.7 copy-start.4
where the time goes:
time: 102 us
  Pallas kernels  95.7 us (94%)
  local copies, waits for them, and re-layouts  6.26 us (6%)
    pallas_call x1, Pallas kernels, body(): pl.pallas_call(functools.partial(kernel, n_row, n_vec), out_shape=jax.Sha...  95.7 us
    unnamed x11, local copies, waits for them, and re-layouts  6.26 us

commit v1 on v0

v1 whole, which is shorter than its diff:
```python
import functools

import jax
import jax.numpy as jnp
from jax import lax
from jax.experimental import pallas as pl
from jax.experimental.pallas import tpu as pltpu
from jax.sharding import PartitionSpec as P

MESH = pl.DeviceIdType.MESH
F32, BF16 = jnp.float32, jnp.bfloat16
FRONTS = 3
PREV = FRONTS
R = 256
H = 128
PACK = 704
NC = 4


def split(x):
    high = x.astype(BF16)
    return high, (x - high.astype(F32)).astype(BF16)


def where(value, target, yes, no):
    return jnp.where(jnp.full(yes.shape, value, jnp.int32) == jnp.full(yes.shape, target, jnp.int32), yes, no)


def mm(a, b):
    dot = functools.partial(jnp.dot, preferred_element_type=F32)
    return dot(a[0], b[0]) + (dot(a[0], b[1]) + dot(a[1], b[0]))


def kernel(
    n_row,
    n_vec,
    slab,
    index_hbm,
    offset_hbm,
    v_hbm,
    s_hbm,
    out,
    index,
    offset,
    w,
    first,
    last,
    bin_,
    din,
    dout,
    bout,
    pad,
    blk,
    sib_blk,
    vb,
    ps,
    pr,
    ms,
    mr,
    xs,
    xr,
    vt_h,
    vt_l,
    v_h,
    v_l,
    s_h,
    s_l,
    in_sem,
    raw_sem,
    p_ssem,
    p_rsem,
    m_ssem,
    m_rsem,
    x_ssem,
    x_rsem,
    z_ssem,
    z_rsem,
    ap_ssem,
    ap_rsem,
    am_ssem,
    am_rsem,
    c_ssem,
    c_rsem,
    d_ssem,
    d_rsem,
    b_ssem,
    b_rsem,
    out_sem,
):
    ny = n_vec // 4
    plus, minus = ny // 2, ny // 2 - 1
    rows = PACK // ny
    wide = w.shape[2]
    row, vec = lax.axis_index("row"), lax.axis_index("vec")
    y, half, core = vec // 4, (vec // 2) % 2, vec % 2
    up = (row, ((y + 1) % ny) * 4 + vec % 4)
    down = (row, ((y + ny - 1) % ny) * 4 + vec % 4)
    sib = (row, vec + 1 - 2 * core)
    across = (row, vec + 2 - 4 * half)
    below = ((row + 1) % n_row, vec)
    above = ((row + n_row - 1) % n_row, vec)
    other = 1 - core

    def remote(src, dst, ssem, rsem, to):
        return pltpu.make_async_remote_copy(
            src_ref=src, dst_ref=dst, send_sem=ssem, recv_sem=rsem, device_id=to, device_id_type=MESH
        )

    stage = [
        pltpu.make_async_copy(v_hbm.at[0, 0, :, pl.ds(0, H)], blk.at[0, pl.ds(0, 512)], in_sem.at[0]),
        pltpu.make_async_copy(v_hbm.at[0, 0, :, pl.ds(H, H)], blk.at[1, pl.ds(0, 512)], in_sem.at[1]),
        pltpu.make_async_copy(s_hbm.at[0, 0, pl.ds(0, 128), pl.ds(0, H)], blk.at[0, pl.ds(512, 128)], in_sem.at[2]),
        pltpu.make_async_copy(s_hbm.at[0, 0, pl.ds(192, 64), pl.ds(H, H)], blk.at[0, pl.ds(640, 64)], in_sem.at[3]),
        pltpu.make_async_copy(s_hbm.at[0, 0, pl.ds(0, 192), pl.ds(H, H)], blk.at[1, pl.ds(512, 192)], in_sem.at[4]),
        pltpu.make_async_copy(index_hbm, index, in_sem.at[5 + 3 * NC]),
        pltpu.make_async_copy(offset_hbm, offset, in_sem.at[6 + 3 * NC]),
    ]
    firsts = [
        pltpu.make_async_copy(slab.at[pl.ds(0, R), pl.ds(c * wide, wide)], first.at[c], in_sem.at[5 + c])
        for c in range(NC)
    ]
    lasts = [
        pltpu.make_async_copy(slab.at[pl.ds(3 * R, R), pl.ds(c * wide, wide)], last.at[c], in_sem.at[5 + NC + c])
        for c in range(NC)
    ]
    loads = [
        pltpu.make_async_copy(slab.at[:, pl.ds(c * wide, wide)], w.at[c], in_sem.at[5 + 2 * NC + c])
        for c in range(NC)
    ]
    for copy in stage + firsts + lasts + loads:
        copy.start()

    barrier = pltpu.get_barrier_semaphore()
    for to in (up, down, sib, across, below, above):
        pl.semaphore_signal(barrier, inc=1, device_id=to, device_id_type=MESH)
    pl.semaphore_wait(barrier, 6)

    for copy in stage:
        copy.wait()
    raw = remote(blk.at[other], sib_blk, raw_sem.at[0], raw_sem.at[1], sib)
    raw.start()

    def d_copy(k, src):
        return remote(src, din.at[k], d_ssem.at[k], d_rsem.at[k], above)

    def b_copy(k, src):
        return remote(src, bin_.at[k], b_ssem.at[k], b_rsem.at[k], below)

    for c in range(NC):
        firsts[c].wait()
        d_copy(c, first.at[c]).start()
        lasts[c].wait()
        b_copy(c, last.at[c]).start()

    roots = [index[f, row] for f in range(FRONTS)]
    chip = [lax.shift_right_logical(root, 1) for root in roots]
    side = [lax.bitwise_and(part, 1) for part in chip]
    line = [lax.shift_right_logical(root, 2) for root in roots]

    def piece(o):
        return pl.ds(pl.multiple_of(o * rows, 8), rows)

    def candidate(f, o):
        return where(roots[f], sib[1], sib_blk[piece(o), :], blk[core, piece(o), :])

    def p_copy(f, s):
        i = f * plus + s
        return remote(ps.at[i], pr.at[i], p_ssem.at[i], p_rsem.at[i], up)

    def m_copy(f, s):
        i = f * minus + s
        return remote(ms.at[i], mr.at[i], m_ssem.at[i], m_rsem.at[i], down)

    def x_copy(f):
        return remote(xs.at[f], xr.at[f], x_ssem.at[f], x_rsem.at[f], across)

    def ap_copy(f, s):
        at = vb.at[f, core, piece((y + ny - s) % ny)]
        return remote(at, at, ap_ssem.at[f * plus + s], ap_rsem.at[f * plus + s], up)

    def ap_wait(f, s):
        at = vb.at[f, core, piece((y + ny - 1 - s) % ny)]
        remote(at, at, ap_ssem.at[f * plus + s], ap_rsem.at[f * plus + s], up).wait_recv()

    def am_copy(f, s):
        at = vb.at[f, core, piece((y + s) % ny)]
        return remote(at, at, am_ssem.at[f * minus + s], am_rsem.at[f * minus + s], down)

    def am_wait(f, s):
        at = vb.at[f, core, piece((y + 1 + s) % ny)]
        remote(at, at, am_ssem.at[f * minus + s], am_rsem.at[f * minus + s], down).wait_recv()

    def c_copy(f, t, o):
        at = vb.at[f, core, piece(o)]
        return remote(at, at, c_ssem.at[f * ny + t], c_rsem.at[f * ny + t], sib)

    def c_wait(f, t, o):
        at = vb.at[f, other, piece(o)]
        remote(at, at, c_ssem.at[f * ny + t], c_rsem.at[f * ny + t], sib).wait_recv()

    def slots():
        yield 0, y
        for s in range(plus):
            yield 1 + s, (y + ny - 1 - s) % ny
        for s in range(minus):
            yield 1 + plus + s, (y + 1 + s) % ny

    def z_copy(f):
        src, dst = vb.at[f, core, piece(y)], vb.at[PREV + f, core, piece(y)]
        return remote(src, dst, z_ssem.at[f], z_rsem.at[f], below)

    def select(f, s):
        mine = candidate(f, (y + plus - s) % ny)
        if s > 0:
            p_copy(f, s - 1).wait_recv()
            mine = where(chip[f], vec // 2, mine, pr[f * plus + s - 1])
        ps[f * plus + s] = mine
        if s < minus:
            back = candidate(f, (y + ny - minus + s) % ny)
            if s > 0:
                m_copy(f, s - 1).wait_recv()
                back = where(chip[f], vec // 2, back, mr[f * minus + s - 1])
            ms[f * minus + s] = back
        p_copy(f, s).start()
        if s < minus:
            m_copy(f, s).start()

    def swap(f):
        p_copy(f, plus - 1).wait_recv()
        m_copy(f, minus - 1).wait_recv()
        got = pr[f * plus + plus - 1]
        for s in range(minus):
            got = where(line[f], (y + 1 + s) % ny, mr[f * minus + minus - 1], got)
        xs[f] = where(chip[f], vec // 2, candidate(f, y), got)
        x_copy(f).start()

    def begin(g):
        if g >= PREV:
            z_copy(g - PREV).wait_recv()
        else:
            x_copy(g).wait_recv()
            vb[g, core, piece(y), :] = where(side[g], half, xs[g], xr[g])
        ap_copy(g, 0).start()
        am_copy(g, 0).start()
        if g < PREV:
            z_copy(g).start()
        c_copy(g, 0, y).start()

    def gather(g, s):
        ap_wait(g, s)
        if s + 1 < plus:
            ap_copy(g, s + 1).start()
        if s < minus:
            am_wait(g, s)
            if s + 1 < minus:
                am_copy(g, s + 1).start()
        c_copy(g, 1 + s, (y + ny - 1 - s) % ny).start()
        if s < minus:
            c_copy(g, 1 + plus + s, (y + 1 + s) % ny).start()

    def whole(g):
        for t, o in slots():
            c_wait(g, t, o)

    delay = {0: 0, PREV: 1, 1: 1, PREV + 1: 2, 2: 3, PREV + 2: 4}

    def tick(t):
        for g, late in delay.items():
            s = t - late - 1
            if s == -1:
                begin(g)
            elif 0 <= s < plus:
                gather(g, s)

    raw.wait_recv()
    for s in range(plus):
        for f in range(FRONTS):
            select(f, s)
    for f in range(FRONTS):
        swap(f)

    def prepare(f):
        for j in range(2):
            block = vb[f, j, 0:512, :]
            v_h[f, :, j * H : (j + 1) * H], v_l[f, :, j * H : (j + 1) * H] = split(block)
            vt_h[f, j * H : (j + 1) * H, :], vt_l[f, j * H : (j + 1) * H, :] = split(block.T)
        upper = lax.broadcasted_iota(jnp.int32, (H, H), 0) <= lax.broadcasted_iota(jnp.int32, (H, H), 1)
        a = jnp.where(upper, vb[f, 0, 512:640, :], 0.0)
        b = vb[f, 1, 512:640, :]
        c = jnp.where(upper, jnp.concatenate([vb[f, 1, 640:704, :], vb[f, 0, 640:704, :]], axis=0), 0.0)
        zero = jnp.zeros((H, H), F32)
        if f >= PREV:
            place, crossing = offset[f - PREV, above[0]], 3 + (n_row - row) // n_row
        for i, j, part in ((0, 0, a), (0, 1, b), (1, 0, zero), (1, 1, c)):
            at = (f, slice(i * H, (i + 1) * H), slice(j * H, (j + 1) * H))
            s_h[at], s_l[at] = split(where(place, crossing, part, zero) if f >= PREV else part)

    for t in range(plus + 1):
        tick(t)
    for copy in loads:
        copy.wait()
    whole(0)
    prepare(0)
    tick(plus + 1)
    whole(PREV)
    prepare(PREV)

    def out_copy(c):
        return pltpu.make_async_copy(w.at[c], out.at[:, pl.ds(c * wide, wide)], out_sem.at[c])

    def edge(f, c, k):
        g = PREV + f
        b, t = split(bin_[k]), split(w[c, 0:R, :])
        inner = mm((vt_h[g, :, 0:R], vt_l[g, :, 0:R]), b) + mm((vt_h[g, :, R : 2 * R], vt_l[g, :, R : 2 * R]), t)
        mixed = split(mm((s_h[g], s_l[g]), split(inner)))
        w[c, 0:R, :] = w[c, 0:R, :] - mm((v_h[g, R : 2 * R, :], v_l[g, R : 2 * R, :]), mixed)

    def own(f, c, k):
        place = offset[f, row]
        parts = [w[c, b * R : (b + 1) * R, :] for b in range(4)] + [din[k]]
        window = [parts[3 + i] for i in range(2)]
        for b in (2, 1, 0):
            window = [where(place, b, parts[b + i], window[i]) for i in range(2)]
        inner = mm((vt_h[f], vt_l[f]), split(jnp.concatenate(window, axis=0)))
        mixed = split(mm((s_h[f], s_l[f]), split(inner)))
        pad[...] = mm((v_h[f], v_l[f]), mixed)
        none = jnp.zeros((R, wide), F32)

        def fresh(b):
            lower = where(place, b - 1, pad[R : 2 * R, :], none) if b > 0 else none
            return w[c, b * R : (b + 1) * R, :] - where(place, b, pad[0:R, :], lower)

        top, bottom = fresh(0), fresh(3)

        @pl.when(k < (FRONTS - 1) * NC)
        def _():
            dout[k] = top
            bout[k] = bottom

        w[c, 0:R, :] = top
        w[c, 3 * R : 4 * R, :] = bottom
        for b in (1, 2):
            w[c, b * R : (b + 1) * R, :] = fresh(b)

        @pl.when(k < (FRONTS - 1) * NC)
        def _():
            d_copy(k + NC, dout.at[k]).start()
            b_copy(k + NC, bout.at[k]).start()

        @pl.when(k >= (FRONTS - 1) * NC)
        def _():
            pltpu.make_async_copy(
                w.at[c], out.at[:, pl.ds(pl.multiple_of(c * wide, wide), wide)], out_sem.at[c]
            ).start()

    def step(k, carry):
        @pl.when(k == 2)
        def _():
            tick(plus + 2)

        @pl.when(k == 4)
        def _():
            tick(plus + 3)
            for g in (1, PREV + 1):
                whole(g)
                prepare(g)

        @pl.when(k == 6)
        def _():
            tick(plus + 4)

        @pl.when(k == 8)
        def _():
            for g in (2, PREV + 2):
                whole(g)
                prepare(g)

        d_copy(k, dout.at[0]).wait_recv()
        b_copy(k, bout.at[0]).wait_recv()
        f, c = k // NC, k % NC
        edge(f, c, k)
        own(f, c, k)
        return carry

    lax.fori_loop(0, FRONTS * NC, step, 0)

    raw.wait_send()
    for f in range(2 * FRONTS):
        if f < FRONTS:
            x_copy(f).wait_send()
            z_copy(f).wait_send()
            for s in range(plus):
                p_copy(f, s).wait_send()
            for s in range(minus):
                m_copy(f, s).wait_send()
        for s in range(plus):
            ap_copy(f, s).wait_send()
        for s in range(minus):
            am_copy(f, s).wait_send()
        for t, o in slots():
            c_copy(f, t, o).wait_send()
    for k in range(FRONTS * NC):
        d_copy(k, dout.at[0]).wait_send()
        b_copy(k, bout.at[0]).wait_send()
    for c in range(NC):
        out_copy(c).wait()


def solution(mesh):
    n_row, n_vec = mesh.shape["row"], mesh.shape["vec"]
    ny = n_vec // 4
    plus, minus = ny // 2, ny // 2 - 1

    def body(vectors, block_index, block_offset, reflector_vectors, reflector_factors):
        wide = vectors.shape[1] // NC
        steps = FRONTS * NC
        dma = pltpu.SemaphoreType.DMA
        hbm = pl.BlockSpec(memory_space=pltpu.HBM)
        vmem = pltpu.VMEM
        rows = PACK // ny
        return pl.pallas_call(
            functools.partial(kernel, n_row, n_vec),
            out_shape=jax.ShapeDtypeStruct(vectors.shape, F32),
            in_specs=[hbm] * 5,
            out_specs=pl.BlockSpec(memory_space=pl.ANY),
            scratch_shapes=[
                pltpu.SMEM((FRONTS, n_row), jnp.int32),
                pltpu.SMEM((FRONTS, n_row), jnp.int32),
                vmem((NC, 4 * R, wide), F32),
                vmem((NC, R, wide), F32),
                vmem((NC, R, wide), F32),
                vmem((steps, R, wide), F32),
                vmem((steps, R, wide), F32),
                vmem((steps - NC, R, wide), F32),
                vmem((steps - NC, R, wide), F32),
                vmem((2 * R, wide), F32),
                vmem((2, PACK, H), F32),
                vmem((PACK, H), F32),
                vmem((2 * FRONTS, 2, PACK, H), F32),
                vmem((FRONTS * plus, rows, H), F32),
                vmem((FRONTS * plus, rows, H), F32),
                vmem((FRONTS * minus, rows, H), F32),
                vmem((FRONTS * minus, rows, H), F32),
                vmem((FRONTS, rows, H), F32),
                vmem((FRONTS, rows, H), F32),
                vmem((2 * FRONTS, R, 2 * R), BF16),
                vmem((2 * FRONTS, R, 2 * R), BF16),
                vmem((2 * FRONTS, 2 * R, R), BF16),
                vmem((2 * FRONTS, 2 * R, R), BF16),
                vmem((2 * FRONTS, R, R), BF16),
                vmem((2 * FRONTS, R, R), BF16),
                dma((7 + 3 * NC,)),
                dma((2,)),
                dma((FRONTS * plus,)),
                dma((FRONTS * plus,)),
                dma((FRONTS * minus,)),
                dma((FRONTS * minus,)),
                dma((FRONTS,)),
                dma((FRONTS,)),
                dma((FRONTS,)),
                dma((FRONTS,)),
                dma((2 * FRONTS * plus,)),
                dma((2 * FRONTS * plus,)),
                dma((2 * FRONTS * minus,)),
                dma((2 * FRONTS * minus,)),
                dma((2 * FRONTS * ny,)),
                dma((2 * FRONTS * ny,)),
                dma((steps,)),
                dma((steps,)),
                dma((steps,)),
                dma((steps,)),
                dma((NC,)),
            ],
            compiler_params=pltpu.CompilerParams(
                collective_id=0, has_side_effects=True, vmem_limit_bytes=48 * 1024 * 1024
            ),
            name="fronts",
        )(
            *(
                pltpu.with_memory_space_constraint(array, pltpu.HBM)
                for array in (vectors, block_index, block_offset, reflector_vectors, reflector_factors)
            )
        )

    return jax.shard_map(
        body,
        mesh=mesh,
        in_specs=(P("row", "vec"), P(), P(), P("row", "vec", None, None), P("row", "vec", None, None)),
        out_specs=P("row", "vec"),
        check_vma=False,
    )
```

time: 102 us -> 89.4 us (0.88); the launches traced: 102 us -> 87.7 us
  Pallas kernels: 95.7 us -> 86.4 us
  local copies, waits for them, and re-layouts: 6.26 us -> 1.32 us
    pallas_call x1, Pallas kernels: 95.7 us -> 86.4 us  [body(): pl.pallas_call(functools.partial(kernel, n_row, n_vec), out_shape=jax.Sha...]
    unnamed x11 -> x1, local copies, waits for them, and re-layouts: 6.26 us -> 1.32 us
where the time goes in v1:
time: 89.4 us; the launch traced here: 87.7 us
  Pallas kernels  86.4 us (97%)
  local copies, waits for them, and re-layouts  1.32 us (1%)
    pallas_call x1, Pallas kernels, body(): pl.pallas_call(functools.partial(kernel, n_row, n_vec), out_shape=jax.Sha...  86.4 us

profile of v1, /device:TPU:1, one launch (start us, length us, event | category | flops | bytes accessed | tf_op | source)
XLA Modules:
  0.0 87.7 jit_solution(18080902759160421081)
XLA Ops:
  0.0 86.4 %fronts.1 = f32[1024,512]{1,0:T(8,128)S(1)} custom-call(f32[1024,512]{1,0:T(8,128)} %slab.1, s32[3,16]{1,0:T(4,128)} %index_hbm.1, s32[3,16]{1,0:T(4,128)} %offset_hbm.1, f32[1,1,512,256]{3,2,1,0:T(8,128)} %v_hbm.1, f32[1,1,256,256]{3,2,1,0:T(8,128)} %s_hbm.1), custom_call_target="tpu_custom_call" | custom-call | tf_op jit(solution)/shard_map/fronts/pallas_call | solution.py:421
  86.4 1.3 %copy.7 = f32[1024,512]{1,0:T(8,128)} copy(f32[1024,512]{1,0:T(8,128)S(1)} %fronts.1) | data formatting | bytes 4194304

commit v2 on v1

--- a/solution.py
+++ b/solution.py
@@ -15,6 +15,11 @@
 H = 128
 PACK = 704
 NC = 4
+
+
+def streams(rows):
+    cut = (rows // 8 + 1) // 2 * 8
+    return ((0, 0, cut), (0, cut, rows - cut), (1, 0, rows), (2, 0, rows))
 
 
 def split(x):
@@ -59,6 +64,8 @@
     mr,
     xs,
     xr,
+    same_r,
+    cross_r,
     vt_h,
     vt_l,
     v_h,
@@ -75,6 +82,10 @@
     x_rsem,
     z_ssem,
     z_rsem,
+    same_ssem,
+    same_rsem,
+    cross_ssem,
+    cross_rsem,
     ap_ssem,
     ap_rsem,
     am_ssem,
@@ -98,7 +109,9 @@
     sib = (row, vec + 1 - 2 * core)
     across = (row, vec + 2 - 4 * half)
     below = ((row + 1) % n_row, vec)
+    across_below = (below[0], across[1])
     above = ((row + n_row - 1) % n_row, vec)
+    across_above = (above[0], across[1])
     other = 1 - core
 
     def remote(src, dst, ssem, rsem, to):
@@ -131,9 +144,9 @@
         copy.start()
 
     barrier = pltpu.get_barrier_semaphore()
-    for to in (up, down, sib, across, below, above):
+    for to in (up, down, sib, across, below, above, across_below, across_above):
         pl.semaphore_signal(barrier, inc=1, device_id=to, device_id_type=MESH)
-    pl.semaphore_wait(barrier, 6)
+    pl.semaphore_wait(barrier, 8)
 
     for copy in stage:
         copy.wait()
@@ -157,46 +170,65 @@
     side = [lax.bitwise_and(part, 1) for part in chip]
     line = [lax.shift_right_logical(root, 2) for root in roots]
 
-    def piece(o):
-        return pl.ds(pl.multiple_of(o * rows, 8), rows)
-
-    def candidate(f, o):
-        return where(roots[f], sib[1], sib_blk[piece(o), :], blk[core, piece(o), :])
-
-    def p_copy(f, s):
-        i = f * plus + s
-        return remote(ps.at[i], pr.at[i], p_ssem.at[i], p_rsem.at[i], up)
-
-    def m_copy(f, s):
-        i = f * minus + s
-        return remote(ms.at[i], mr.at[i], m_ssem.at[i], m_rsem.at[i], down)
-
-    def x_copy(f):
-        return remote(xs.at[f], xr.at[f], x_ssem.at[f], x_rsem.at[f], across)
-
-    def ap_copy(f, s):
-        at = vb.at[f, core, piece((y + ny - s) % ny)]
-        return remote(at, at, ap_ssem.at[f * plus + s], ap_rsem.at[f * plus + s], up)
-
-    def ap_wait(f, s):
-        at = vb.at[f, core, piece((y + ny - 1 - s) % ny)]
-        remote(at, at, ap_ssem.at[f * plus + s], ap_rsem.at[f * plus + s], up).wait_recv()
-
-    def am_copy(f, s):
-        at = vb.at[f, core, piece((y + s) % ny)]
-        return remote(at, at, am_ssem.at[f * minus + s], am_rsem.at[f * minus + s], down)
-
-    def am_wait(f, s):
-        at = vb.at[f, core, piece((y + 1 + s) % ny)]
-        remote(at, at, am_ssem.at[f * minus + s], am_rsem.at[f * minus + s], down).wait_recv()
-
-    def c_copy(f, t, o):
-        at = vb.at[f, core, piece(o)]
-        return remote(at, at, c_ssem.at[f * ny + t], c_rsem.at[f * ny + t], sib)
-
-    def c_wait(f, t, o):
-        at = vb.at[f, other, piece(o)]
-        remote(at, at, c_ssem.at[f * ny + t], c_rsem.at[f * ny + t], sib).wait_recv()
+    parts = streams(rows)
+    n_streams = len(parts)
+    above_side = lax.bitwise_and(lax.shift_right_logical(index[0, above[0]], 1), 1)
+
+    def piece(q, o):
+        lo, n = parts[q % n_streams][1:]
+        return pl.ds(pl.multiple_of(o * rows + lo, 8), n)
+
+    def part(q):
+        return pl.ds(*parts[q % n_streams][1:])
+
+    def front(q):
+        return parts[q % n_streams][0] + PREV * (q // n_streams)
+
+    def candidate(q, o):
+        return where(roots[front(q)], sib[1], sib_blk[piece(q, o), :], blk[core, piece(q, o), :])
+
+    def p_copy(q, s):
+        f, i = front(q), q * plus + s
+        at = f * plus + s
+        return remote(ps.at[at, part(q)], pr.at[at, part(q)], p_ssem.at[i], p_rsem.at[i], up)
+
+    def m_copy(q, s):
+        f, i = front(q), q * minus + s
+        at = f * minus + s
+        return remote(ms.at[at, part(q)], mr.at[at, part(q)], m_ssem.at[i], m_rsem.at[i], down)
+
+    def x_copy(q):
+        return remote(xs.at[front(q), part(q)], xr.at[front(q), part(q)], x_ssem.at[q], x_rsem.at[q], across)
+
+    def same_copy(q):
+        return remote(xs.at[0, part(q)], same_r.at[part(q)], same_ssem.at[q], same_rsem.at[q], below)
+
+    def cross_copy(q):
+        return remote(xs.at[0, part(q)], cross_r.at[part(q)], cross_ssem.at[q], cross_rsem.at[q], across_below)
+
+    def ap_copy(q, s):
+        at = vb.at[front(q), core, piece(q, (y + ny - s) % ny)]
+        return remote(at, at, ap_ssem.at[q * plus + s], ap_rsem.at[q * plus + s], up)
+
+    def ap_wait(q, s):
+        at = vb.at[front(q), core, piece(q, (y + ny - 1 - s) % ny)]
+        remote(at, at, ap_ssem.at[q * plus + s], ap_rsem.at[q * plus + s], up).wait_recv()
+
+    def am_copy(q, s):
+        at = vb.at[front(q), core, piece(q, (y + s) % ny)]
+        return remote(at, at, am_ssem.at[q * minus + s], am_rsem.at[q * minus + s], down)
+
+    def am_wait(q, s):
+        at = vb.at[front(q), core, piece(q, (y + 1 + s) % ny)]
+        remote(at, at, am_ssem.at[q * minus + s], am_rsem.at[q * minus + s], down).wait_recv()
+
+    def c_copy(q, t, o):
+        at = vb.at[front(q), core, piece(q, o)]
+        return remote(at, at, c_ssem.at[q * ny + t], c_rsem.at[q * ny + t], sib)
+
+    def c_wait(q, t, o):
+        at = vb.at[front(q), other, piece(q, o)]
+        remote(at, at, c_ssem.at[q * ny + t], c_rsem.at[q * ny + t], sib).wait_recv()
 
     def slots():
         yield 0, y
@@ -205,79 +237,92 @@
         for s in range(minus):
             yield 1 + plus + s, (y + 1 + s) % ny
 
-    def z_copy(f):
-        src, dst = vb.at[f, core, piece(y)], vb.at[PREV + f, core, piece(y)]
-        return remote(src, dst, z_ssem.at[f], z_rsem.at[f], below)
-
-    def select(f, s):
-        mine = candidate(f, (y + plus - s) % ny)
+    def z_copy(q):
+        f = front(q)
+        src, dst = vb.at[f, core, piece(q, y)], vb.at[PREV + f, core, piece(q, y)]
+        return remote(src, dst, z_ssem.at[q], z_rsem.at[q], below)
+
+    def select(q, s):
+        f = front(q)
+        mine = candidate(q, (y + plus - s) % ny)
         if s > 0:
-            p_copy(f, s - 1).wait_recv()
-            mine = where(chip[f], vec // 2, mine, pr[f * plus + s - 1])
-        ps[f * plus + s] = mine
+            p_copy(q, s - 1).wait_recv()
+            mine = where(chip[f], vec // 2, mine, pr[f * plus + s - 1, part(q), :])
+        ps[f * plus + s, part(q), :] = mine
         if s < minus:
-            back = candidate(f, (y + ny - minus + s) % ny)
+            back = candidate(q, (y + ny - minus + s) % ny)
             if s > 0:
-                m_copy(f, s - 1).wait_recv()
-                back = where(chip[f], vec // 2, back, mr[f * minus + s - 1])
-            ms[f * minus + s] = back
-        p_copy(f, s).start()
+                m_copy(q, s - 1).wait_recv()
+                back = where(chip[f], vec // 2, back, mr[f * minus + s - 1, part(q), :])
+            ms[f * minus + s, part(q), :] = back
+        p_copy(q, s).start()
         if s < minus:
-            m_copy(f, s).start()
-
-    def swap(f):
-        p_copy(f, plus - 1).wait_recv()
-        m_copy(f, minus - 1).wait_recv()
-        got = pr[f * plus + plus - 1]
+            m_copy(q, s).start()
+
+    def swap(q):
+        f = front(q)
+        p_copy(q, plus - 1).wait_recv()
+        m_copy(q, minus - 1).wait_recv()
+        got = pr[f * plus + plus - 1, part(q), :]
         for s in range(minus):
-            got = where(line[f], (y + 1 + s) % ny, mr[f * minus + minus - 1], got)
-        xs[f] = where(chip[f], vec // 2, candidate(f, y), got)
-        x_copy(f).start()
-
-    def begin(g):
-        if g >= PREV:
-            z_copy(g - PREV).wait_recv()
+            got = where(line[f], (y + 1 + s) % ny, mr[f * minus + minus - 1, part(q), :], got)
+        xs[f, part(q), :] = where(chip[f], vec // 2, candidate(q, y), got)
+        x_copy(q).start()
+        if f == 0:
+            same_copy(q).start()
+            cross_copy(q).start()
+
+    def begin(q):
+        f = front(q)
+        if q < n_streams:
+            x_copy(q).wait_recv()
+            vb[f, core, piece(q, y), :] = where(side[f], half, xs[f, part(q), :], xr[f, part(q), :])
+        elif f == PREV:
+            same_copy(q - n_streams).wait_recv()
+            cross_copy(q - n_streams).wait_recv()
+            vb[f, core, piece(q, y), :] = where(above_side, half, same_r[part(q), :], cross_r[part(q), :])
         else:
-            x_copy(g).wait_recv()
-            vb[g, core, piece(y), :] = where(side[g], half, xs[g], xr[g])
-        ap_copy(g, 0).start()
-        am_copy(g, 0).start()
-        if g < PREV:
-            z_copy(g).start()
-        c_copy(g, 0, y).start()
-
-    def gather(g, s):
-        ap_wait(g, s)
+            z_copy(q - n_streams).wait_recv()
+        ap_copy(q, 0).start()
+        am_copy(q, 0).start()
+        if 0 < f < PREV:
+            z_copy(q).start()
+        c_copy(q, 0, y).start()
+
+    def gather(q, s):
+        ap_wait(q, s)
         if s + 1 < plus:
-            ap_copy(g, s + 1).start()
+            ap_copy(q, s + 1).start()
         if s < minus:
-            am_wait(g, s)
+            am_wait(q, s)
             if s + 1 < minus:
-                am_copy(g, s + 1).start()
-        c_copy(g, 1 + s, (y + ny - 1 - s) % ny).start()
+                am_copy(q, s + 1).start()
+        c_copy(q, 1 + s, (y + ny - 1 - s) % ny).start()
         if s < minus:
-            c_copy(g, 1 + plus + s, (y + 1 + s) % ny).start()
+            c_copy(q, 1 + plus + s, (y + 1 + s) % ny).start()
 
     def whole(g):
-        for t, o in slots():
-            c_wait(g, t, o)
-
-    delay = {0: 0, PREV: 1, 1: 1, PREV + 1: 2, 2: 3, PREV + 2: 4}
+        for q in range(2 * n_streams):
+            if front(q) == g:
+                for t, o in slots():
+                    c_wait(q, t, o)
+
+    delay = {0: 0, 1: 0, 4: 0, 5: 0, 2: 1, 6: 2, 3: 3, 7: 4}
 
     def tick(t):
-        for g, late in delay.items():
+        for q, late in delay.items():
             s = t - late - 1
             if s == -1:
-                begin(g)
+                begin(q)
             elif 0 <= s < plus:
-                gather(g, s)
+                gather(q, s)
 
     raw.wait_recv()
     for s in range(plus):
-        for f in range(FRONTS):
-            select(f, s)
-    for f in range(FRONTS):
-        swap(f)
+        for q in range(n_streams):
+            select(q, s)
+    for q in range(n_streams):
+        swap(q)
 
     def prepare(f):
         for j in range(2):
@@ -301,7 +346,6 @@
         copy.wait()
     whole(0)
     prepare(0)
-    tick(plus + 1)
     whole(PREV)
     prepare(PREV)
 
@@ -354,7 +398,11 @@
             ).start()
 
     def step(k, carry):
-        @pl.when(k == 2)
+        @pl.when(k == 1)
+        def _():
+            tick(plus + 1)
+
+        @pl.when(k == 3)
         def _():
             tick(plus + 2)
 
@@ -385,20 +433,24 @@
     lax.fori_loop(0, FRONTS * NC, step, 0)
 
     raw.wait_send()
-    for f in range(2 * FRONTS):
-        if f < FRONTS:
-            x_copy(f).wait_send()
-            z_copy(f).wait_send()
+    for q in range(2 * n_streams):
+        if q < n_streams:
+            x_copy(q).wait_send()
+            if front(q) == 0:
+                same_copy(q).wait_send()
+                cross_copy(q).wait_send()
+            else:
+                z_copy(q).wait_send()
             for s in range(plus):
-                p_copy(f, s).wait_send()
+                p_copy(q, s).wait_send()
             for s in range(minus):
-                m_copy(f, s).wait_send()
+                m_copy(q, s).wait_send()
         for s in range(plus):
-            ap_copy(f, s).wait_send()
+            ap_copy(q, s).wait_send()
         for s in range(minus):
-            am_copy(f, s).wait_send()
+            am_copy(q, s).wait_send()
         for t, o in slots():
-            c_copy(f, t, o).wait_send()
+            c_copy(q, t, o).wait_send()
     for k in range(FRONTS * NC):
         d_copy(k, dout.at[0]).wait_send()
         b_copy(k, bout.at[0]).wait_send()
@@ -443,6 +495,8 @@
                 vmem((FRONTS * minus, rows, H), F32),
                 vmem((FRONTS, rows, H), F32),
                 vmem((FRONTS, rows, H), F32),
+                vmem((rows, H), F32),
+                vmem((rows, H), F32),
                 vmem((2 * FRONTS, R, 2 * R), BF16),
                 vmem((2 * FRONTS, R, 2 * R), BF16),
                 vmem((2 * FRONTS, 2 * R, R), BF16),
@@ -451,20 +505,24 @@
                 vmem((2 * FRONTS, R, R), BF16),
                 dma((7 + 3 * NC,)),
                 dma((2,)),
-                dma((FRONTS * plus,)),
-                dma((FRONTS * plus,)),
-                dma((FRONTS * minus,)),
-                dma((FRONTS * minus,)),
-                dma((FRONTS,)),
-                dma((FRONTS,)),
-                dma((FRONTS,)),
-                dma((FRONTS,)),
-                dma((2 * FRONTS * plus,)),
-                dma((2 * FRONTS * plus,)),
-                dma((2 * FRONTS * minus,)),
-                dma((2 * FRONTS * minus,)),
-                dma((2 * FRONTS * ny,)),
-                dma((2 * FRONTS * ny,)),
+                dma((4 * plus,)),
+                dma((4 * plus,)),
+                dma((4 * minus,)),
+                dma((4 * minus,)),
+                dma((4,)),
+                dma((4,)),
+                dma((4,)),
+                dma((4,)),
+                dma((2,)),
+                dma((2,)),
+                dma((2,)),
+                dma((2,)),
+                dma((8 * plus,)),
+                dma((8 * plus,)),
+                dma((8 * minus,)),
+                dma((8 * minus,)),
+                dma((8 * ny,)),
+                dma((8 * ny,)),
                 dma((steps,)),
                 dma((steps,)),
                 dma((steps,)),

time: 89.4 us -> 86 us (0.962)
  Pallas kernels: 86.4 us -> 83.8 us
    pallas_call x1, Pallas kernels: 86.4 us -> 83.8 us  [body(): pl.pallas_call(functools.partial(kernel, n_row, n_vec), out_shape=jax.Sha...]
where the time goes in v2:
time: 86 us; the launch traced here: 85.1 us
  Pallas kernels  83.8 us (97%)
  local copies, waits for them, and re-layouts  1.32 us (2%)
    pallas_call x1, Pallas kernels, body(): pl.pallas_call(functools.partial(kernel, n_row, n_vec), out_shape=jax.Sha...  83.8 us

profile of v2, /device:TPU:1, one launch (start us, length us, event | category | flops | bytes accessed | tf_op | source)
XLA Modules:
  0.0 85.1 jit_solution(2860935617437275147)
XLA Ops:
  0.0 83.8 %fronts.1 = f32[1024,512]{1,0:T(8,128)S(1)} custom-call(f32[1024,512]{1,0:T(8,128)} %slab.1, s32[3,16]{1,0:T(4,128)} %index_hbm.1, s32[3,16]{1,0:T(4,128)} %offset_hbm.1, f32[1,1,512,256]{3,2,1,0:T(8,128)} %v_hbm.1, f32[1,1,256,256]{3,2,1,0:T(8,128)} %s_hbm.1), custom_call_target="tpu_custom_call" | custom-call | tf_op jit(solution)/shard_map/fronts/pallas_call | solution.py:473
  83.8 1.3 %copy.7 = f32[1024,512]{1,0:T(8,128)} copy(f32[1024,512]{1,0:T(8,128)S(1)} %fronts.1) | data formatting | bytes 4194304

commit v3 on v2

--- a/solution.py
+++ b/solution.py
@@ -154,10 +154,10 @@
     raw.start()
 
     def d_copy(k, src):
-        return remote(src, din.at[k], d_ssem.at[k], d_rsem.at[k], above)
+        return remote(src, din.at[k], d_ssem.at[0], d_rsem.at[k], above)
 
     def b_copy(k, src):
-        return remote(src, bin_.at[k], b_ssem.at[k], b_rsem.at[k], below)
+        return remote(src, bin_.at[k], b_ssem.at[0], b_rsem.at[k], below)
 
     for c in range(NC):
         firsts[c].wait()
@@ -190,15 +190,15 @@
     def p_copy(q, s):
         f, i = front(q), q * plus + s
         at = f * plus + s
-        return remote(ps.at[at, part(q)], pr.at[at, part(q)], p_ssem.at[i], p_rsem.at[i], up)
+        return remote(ps.at[at, part(q)], pr.at[at, part(q)], p_ssem.at[0], p_rsem.at[i], up)
 
     def m_copy(q, s):
         f, i = front(q), q * minus + s
         at = f * minus + s
-        return remote(ms.at[at, part(q)], mr.at[at, part(q)], m_ssem.at[i], m_rsem.at[i], down)
+        return remote(ms.at[at, part(q)], mr.at[at, part(q)], m_ssem.at[0], m_rsem.at[i], down)
 
     def x_copy(q):
-        return remote(xs.at[front(q), part(q)], xr.at[front(q), part(q)], x_ssem.at[q], x_rsem.at[q], across)
+        return remote(xs.at[front(q), part(q)], xr.at[front(q), part(q)], x_ssem.at[0], x_rsem.at[q], across)
 
     def same_copy(q):
         return remote(xs.at[0, part(q)], same_r.at[part(q)], same_ssem.at[q], same_rsem.at[q], below)
@@ -208,34 +208,23 @@
 
     def ap_copy(q, s):
         at = vb.at[front(q), core, piece(q, (y + ny - s) % ny)]
-        return remote(at, at, ap_ssem.at[q * plus + s], ap_rsem.at[q * plus + s], up)
+        return remote(at, at, ap_ssem.at[0], ap_rsem.at[q * plus + s], up)
 
     def ap_wait(q, s):
         at = vb.at[front(q), core, piece(q, (y + ny - 1 - s) % ny)]
-        remote(at, at, ap_ssem.at[q * plus + s], ap_rsem.at[q * plus + s], up).wait_recv()
+        remote(at, at, ap_ssem.at[0], ap_rsem.at[q * plus + s], up).wait_recv()
 
     def am_copy(q, s):
         at = vb.at[front(q), core, piece(q, (y + s) % ny)]
-        return remote(at, at, am_ssem.at[q * minus + s], am_rsem.at[q * minus + s], down)
+        return remote(at, at, am_ssem.at[0], am_rsem.at[q * minus + s], down)
 
     def am_wait(q, s):
         at = vb.at[front(q), core, piece(q, (y + 1 + s) % ny)]
-        remote(at, at, am_ssem.at[q * minus + s], am_rsem.at[q * minus + s], down).wait_recv()
+        remote(at, at, am_ssem.at[0], am_rsem.at[q * minus + s], down).wait_recv()
 
     def c_copy(q, t, o):
         at = vb.at[front(q), core, piece(q, o)]
-        return remote(at, at, c_ssem.at[q * ny + t], c_rsem.at[q * ny + t], sib)
-
-    def c_wait(q, t, o):
-        at = vb.at[front(q), other, piece(q, o)]
-        remote(at, at, c_ssem.at[q * ny + t], c_rsem.at[q * ny + t], sib).wait_recv()
-
-    def slots():
-        yield 0, y
-        for s in range(plus):
-            yield 1 + s, (y + ny - 1 - s) % ny
-        for s in range(minus):
-            yield 1 + plus + s, (y + 1 + s) % ny
+        return remote(at, at, c_ssem.at[0], c_rsem.at[front(q)], sib)
 
     def z_copy(q):
         f = front(q)
@@ -302,10 +291,8 @@
             c_copy(q, 1 + plus + s, (y + 1 + s) % ny).start()
 
     def whole(g):
-        for q in range(2 * n_streams):
-            if front(q) == g:
-                for t, o in slots():
-                    c_wait(q, t, o)
+        view = vb.at[g, other]
+        remote(view, view, c_ssem.at[0], c_rsem.at[g], sib).wait_recv()
 
     delay = {0: 0, 1: 0, 4: 0, 5: 0, 2: 1, 6: 2, 3: 3, 7: 4}
 
@@ -433,27 +420,23 @@
     lax.fori_loop(0, FRONTS * NC, step, 0)
 
     raw.wait_send()
-    for q in range(2 * n_streams):
-        if q < n_streams:
-            x_copy(q).wait_send()
-            if front(q) == 0:
-                same_copy(q).wait_send()
-                cross_copy(q).wait_send()
-            else:
-                z_copy(q).wait_send()
-            for s in range(plus):
-                p_copy(q, s).wait_send()
-            for s in range(minus):
-                m_copy(q, s).wait_send()
-        for s in range(plus):
-            ap_copy(q, s).wait_send()
-        for s in range(minus):
-            am_copy(q, s).wait_send()
-        for t, o in slots():
-            c_copy(q, t, o).wait_send()
-    for k in range(FRONTS * NC):
-        d_copy(k, dout.at[0]).wait_send()
-        b_copy(k, bout.at[0]).wait_send()
+    def sent(view, ssem, rsem, to):
+        remote(view, view, ssem, rsem, to).wait_send()
+
+    for q in range(n_streams):
+        if front(q) == 0:
+            same_copy(q).wait_send()
+            cross_copy(q).wait_send()
+        else:
+            z_copy(q).wait_send()
+    sent(xs, x_ssem.at[0], x_rsem.at[0], across)
+    sent(ps, p_ssem.at[0], p_rsem.at[0], up)
+    sent(ms, m_ssem.at[0], m_rsem.at[0], down)
+    sent(vb.at[:, core, pl.ds(0, plus * rows)], ap_ssem.at[0], ap_rsem.at[0], up)
+    sent(vb.at[:, core, pl.ds(0, minus * rows)], am_ssem.at[0], am_rsem.at[0], down)
+    sent(vb.at[:, core], c_ssem.at[0], c_rsem.at[0], sib)
+    sent(din, d_ssem.at[0], d_rsem.at[0], above)
+    sent(bin_, b_ssem.at[0], b_rsem.at[0], below)
     for c in range(NC):
         out_copy(c).wait()
 
@@ -505,11 +488,11 @@
                 vmem((2 * FRONTS, R, R), BF16),
                 dma((7 + 3 * NC,)),
                 dma((2,)),
+                dma((1,)),
                 dma((4 * plus,)),
-                dma((4 * plus,)),
+                dma((1,)),
                 dma((4 * minus,)),
-                dma((4 * minus,)),
-                dma((4,)),
+                dma((1,)),
                 dma((4,)),
                 dma((4,)),
                 dma((4,)),
@@ -517,15 +500,15 @@
                 dma((2,)),
                 dma((2,)),
                 dma((2,)),
+                dma((1,)),
                 dma((8 * plus,)),
-                dma((8 * plus,)),
+                dma((1,)),
                 dma((8 * minus,)),
-                dma((8 * minus,)),
-                dma((8 * ny,)),
-                dma((8 * ny,)),
+                dma((1,)),
+                dma((2 * FRONTS,)),
+                dma((1,)),
                 dma((steps,)),
-                dma((steps,)),
-                dma((steps,)),
+                dma((1,)),
                 dma((steps,)),
                 dma((NC,)),
             ],

time: 86 us -> 83.7 us (0.973)
  Pallas kernels: 83.8 us -> 81.5 us
    pallas_call x1, Pallas kernels: 83.8 us -> 81.5 us  [body(): pl.pallas_call(functools.partial(kernel, n_row, n_vec), out_shape=jax.Sha...]
where the time goes in v3:
time: 83.7 us; the launch traced here: 82.8 us
  Pallas kernels  81.5 us (97%)
  local copies, waits for them, and re-layouts  1.32 us (2%)
    pallas_call x1, Pallas kernels, body(): pl.pallas_call(functools.partial(kernel, n_row, n_vec), out_shape=jax.Sha...  81.5 us

profile of v3, /device:TPU:1, one launch (start us, length us, event | category | flops | bytes accessed | tf_op | source)
XLA Modules:
  0.0 82.8 jit_solution(8936757052045902898)
XLA Ops:
  0.0 81.5 %fronts.1 = f32[1024,512]{1,0:T(8,128)S(1)} custom-call(f32[1024,512]{1,0:T(8,128)} %slab.1, s32[3,16]{1,0:T(4,128)} %index_hbm.1, s32[3,16]{1,0:T(4,128)} %offset_hbm.1, f32[1,1,512,256]{3,2,1,0:T(8,128)} %v_hbm.1, f32[1,1,256,256]{3,2,1,0:T(8,128)} %s_hbm.1), custom_call_target="tpu_custom_call" | custom-call | tf_op jit(solution)/shard_map/fronts/pallas_call | solution.py:456
  81.5 1.3 %copy.7 = f32[1024,512]{1,0:T(8,128)} copy(f32[1024,512]{1,0:T(8,128)S(1)} %fronts.1) | data formatting | bytes 4194304
